TPU v7x, 32 devices: a whole 2x2x4 slice. The times are simulated.
32 devices in a mesh: vol: 4 (over y, x), orient: 4 (over z), dp: 2 (over core).
Axes of the slice: x: 2, y: 2, z: 4, core: 2. Of those that a mesh axis runs over, the one named last changes fastest.
Arguments:
- volume: float32 [128, 65, 2, 8, 128], P('vol'), may hold values from -6 to 6
- weight_bank: float32 [64, 128, 128], replicated, may hold values from -3 to 3
- tile_slab: int32 [128, 65, 1], P(('vol', 'orient')), may hold values from 0 to 3; in each aligned block of 520 rows (0 to 519, 520 to 1039, ..., all dimensions but the last counted through in order) at most 260 rows name the same one
- tile_plane: int32 [128, 65], P(('vol', 'orient')), may hold values from 0 to 31
- tile_weight: int32 [128, 65], P(('vol', 'orient')), may hold values from 0 to 63
- particles: float32 [256, 65, 2, 128], P('dp'), may hold values from -6 to 6
- ctf: float32 [256, 65, 128], P('dp'), may hold values from -1 to 1
- noise_weight: float32 [65, 128], replicated, may hold values from 0.002 to 0.11
- offsets: int32 [256, 2], P('dp'), may hold values from -3 to 3
- earlier_class: int32 [256], P('dp'), may hold values from 0 to 7
- pose_free_term: float32 [256], P('dp'), may hold values from -160 to 160
Outputs:
- numerator: float32 [128, 65, 3, 8, 128], P(('vol', 'orient', 'dp'))
- posterior: float32 [256, 8], P('dp')
- log_evidence: float32 [256], P('dp')
Inputs may be any that keep to these rules, and one draw needn't show every extreme that they name: `tile_slab`: among the 65 tiles of the 8 poses of one device at most 260 name one slab, and in every draw some device's tiles name some slab exactly 260 times.
All inputs are finite; a program needn't handle non-finite values.
Results may differ from a plain program's by a relative error of at most 0.0003.
Values sent between devices are 32-bit elements; how exact they have to be, the bound alone decides.
No kernel may reach another device: no remote copies, remote signals or barrier semaphores. Data moves between devices by JAX's collectives and lax.ppermute only.
A program may use at most 192 MiB of HBM per device.

v0:
```python
import math
import jax
import jax.numpy as jnp
from jax import lax
from jax.sharding import PartitionSpec as P

SIDE = 128
NTRANS = 9
PREVIOUS_REWARD = 1.5
PRECISE = lax.Precision.HIGHEST


def pixel_frequencies(image_side, tile_count, tile_width):
    pixel = jnp.arange(tile_count * tile_width, dtype=jnp.int32).reshape(tile_count, tile_width)
    half_width = image_side // 2 + 1
    freq_x = pixel % half_width
    row_index = pixel // half_width
    freq_y = jnp.where(row_index < image_side // 2, row_index, row_index - image_side)
    return (freq_x, freq_y)


def moved_images(images, offsets, freq_x, freq_y, image_side, trans_step):
    shift_horizontal = offsets[:, 0] + (trans_step % 3 - 1)
    move_y = offsets[:, 1] + (trans_step // 3 - 1)
    turns = jnp.mod(
        freq_x[None] * shift_horizontal[:, None, None] + freq_y[None] * move_y[:, None, None],
        image_side,
    )
    phase_angle = turns.astype(jnp.float32) * (2.0 * math.pi / image_side)
    cosine = jnp.cos(phase_angle)
    sine_part = jnp.sin(phase_angle)
    real_part = images[:, :, 0, :]
    imag_part = images[:, :, 1, :]
    return jnp.stack(
        [real_part * cosine + imag_part * sine_part, imag_part * cosine - real_part * sine_part],
        axis=2,
    )


def project_tiles(blocks, weight_bank, chosen):
    matrices = weight_bank[chosen]
    return jnp.einsum("nckr,nrq->nckq", blocks, matrices, precision=PRECISE)


def back_project(tile_rows, weight_bank, chosen):
    matrices = weight_bank[chosen]
    return jnp.einsum("nmkq,nrq->nmkr", tile_rows, matrices, precision=PRECISE)


def shards(
    volume,
    weight_bank,
    tile_slab,
    tile_plane,
    tile_weight,
    particles,
    ctf,
    noise_weight,
    offsets,
    earlier_class,
    pose_free_term,
):
    slab_count = lax.axis_size("vol")
    pose_local = tile_plane.shape[0]
    tile_count = tile_plane.shape[1]
    tile_width = particles.shape[3]
    class_labels = volume.shape[3]
    planes = volume.shape[0]
    capacity = max(2, 2 * pose_local * tile_count // slab_count)
    row_total = pose_local * tile_count
    slab_of = tile_slab[:, :, 0].reshape(row_total)
    plane_of = tile_plane.reshape(row_total)
    chosen = tile_weight.reshape(row_total)
    target = (slab_of[:, None] == jnp.arange(slab_count, dtype=jnp.int32)[None]).astype(jnp.int32)
    slot_rank = jnp.sum((jnp.cumsum(target, axis=0) - 1) * target, axis=1)
    slot_index = slab_of * capacity + slot_rank
    local_cell = plane_of * tile_count + jnp.tile(
        jnp.arange(tile_count, dtype=jnp.int32), pose_local
    )
    request = jnp.full((slab_count * capacity,), -1, jnp.int32).at[slot_index].set(local_cell)
    request = request.reshape(slab_count, capacity)
    flat_volume = volume.reshape(planes * tile_count, 2, class_labels, tile_width)

    def project_group(item_pair):
        return project_tiles(item_pair[0], weight_bank, item_pair[1])

    def spread_group(item_pair):
        return back_project(item_pair[0], weight_bank, item_pair[1])

    weight_request = jnp.zeros((slab_count * capacity,), jnp.int32).at[slot_index].set(chosen)
    weight_request = weight_request.reshape(slab_count, capacity)
    incoming, incoming_weight = (
        lax.all_to_all(request, "vol", split_axis=0, concat_axis=0, tiled=True),
        lax.all_to_all(weight_request, "vol", split_axis=0, concat_axis=0, tiled=True),
    )
    is_valid = incoming >= 0
    picked = flat_volume[jnp.maximum(incoming, 0)]
    blocks = jnp.where(is_valid[..., None, None, None], picked, 0.0)
    pieces = lax.map(project_group, (blocks, incoming_weight))
    returned = lax.all_to_all(pieces, "vol", split_axis=0, concat_axis=0, tiled=True)
    slices = returned.reshape(slab_count * capacity, 2, class_labels, tile_width)[slot_index]
    slices = slices.reshape(pose_local, tile_count, 2, class_labels, tile_width)
    freq_x, freq_y = pixel_frequencies(SIDE, tile_count, tile_width)
    ctf_noise = noise_weight[None] * ctf
    power = jnp.sum(slices * slices, axis=2)
    norm_term = jnp.einsum("itq,ptkq->ikp", ctf_noise * ctf, power, precision=PRECISE)
    trans_steps = jnp.arange(NTRANS, dtype=jnp.int32)

    def score_step(trans_step):
        moved = moved_images(particles, offsets, freq_x, freq_y, SIDE, trans_step)
        return jnp.einsum(
            "itcq,ptckq->ikp", ctf_noise[:, :, None, :] * moved, slices, precision=PRECISE
        )

    cross_term = lax.map(score_step, trans_steps)
    earlier_class_term = jnp.where(
        earlier_class[:, None] == jnp.arange(class_labels, dtype=jnp.int32)[None],
        PREVIOUS_REWARD,
        0.0,
    )
    earlier_class_term = earlier_class_term + pose_free_term[:, None]
    scores = 2.0 * cross_term - norm_term[None] + earlier_class_term[None, :, :, None]
    peak_value = lax.pmax(jnp.max(scores, axis=(0, 2, 3)), ("vol", "orient"))
    exp_scores = jnp.exp(scores - peak_value[None, :, None, None])
    class_mass = lax.psum(jnp.sum(exp_scores, axis=(0, 3)), ("vol", "orient"))
    mass_total = jnp.sum(class_mass, axis=1)
    posterior = class_mass / mass_total[:, None]
    evidence = peak_value + jnp.log(mass_total)
    pose_count = pose_local * lax.axis_size("vol") * lax.axis_size("orient")
    post_share = exp_scores * (pose_count / mass_total)[None, :, None, None]

    def add_step(running, item_pair):
        trans_step, share_step = item_pair
        moved = moved_images(particles, offsets, freq_x, freq_y, SIDE, trans_step)
        term = jnp.einsum(
            "ikp,itcq->ptckq", share_step, ctf[:, :, None, :] * moved, precision=PRECISE
        )
        return (running + term, None)

    start = jnp.zeros((pose_local, tile_count, 2, class_labels, tile_width), jnp.float32)
    data_rows = lax.scan(add_step, start, (trans_steps, post_share))[0]
    weight_rows = jnp.einsum(
        "ikp,itq->ptkq", jnp.sum(post_share, axis=0), ctf * ctf, precision=PRECISE
    )
    slice_rows = jnp.concatenate([data_rows, weight_rows[:, :, None]], axis=2)
    outgoing = jnp.zeros((slab_count * capacity, 3, class_labels, tile_width), jnp.float32)
    outgoing = outgoing.at[slot_index].set(
        slice_rows.reshape(row_total, 3, class_labels, tile_width)
    )
    outgoing = outgoing.reshape(slab_count, capacity, 3, class_labels, tile_width)
    arrived_rows = lax.all_to_all(outgoing, "vol", split_axis=0, concat_axis=0, tiled=True)
    arrived = lax.map(spread_group, (arrived_rows, incoming_weight))
    cell_index = jnp.maximum(incoming, 0).reshape(-1)
    accumulated = jnp.zeros((planes * tile_count, 3, class_labels, tile_width), jnp.float32)
    accumulated = accumulated.at[cell_index].add(arrived.reshape(-1, 3, class_labels, tile_width))
    accumulated = accumulated.reshape(planes, tile_count, 3, class_labels, tile_width)
    numerator = lax.psum_scatter(accumulated, ("orient", "dp"), scatter_dimension=0, tiled=True)
    return (numerator, posterior, evidence)


def solution(mesh):
    in_specs = (
        P("vol", None, None, None, None),
        P(),
        P(("vol", "orient"), None, None),
        P(("vol", "orient"), None),
        P(("vol", "orient"), None),
        P("dp", None, None, None),
        P("dp", None, None),
        P(),
        P("dp", None),
        P("dp"),
        P("dp"),
    )
    out_specs = (P(("vol", "orient", "dp"), None, None, None, None), P("dp", None), P("dp"))
    return jax.shard_map(shards, mesh=mesh, in_specs=in_specs, out_specs=out_specs, check_vma=False)
```

profile of v0, /device:TPU:0, one launch (start us, length us, event | category | flops | bytes accessed | tf_op | source)
XLA Modules:
  0.0 1769.5 jit_solution(17040077565508846166)
XLA Ops:
  52.4 129.7 %while.52 = (s32[]{:T(128)}, f32[4,260,2,8,128]{4,3,2,1,0:T(8,128)}, f32[4,260,2,8,128]{4,3,2,1,0:T(8,128)}, s32[4,260]{1,0:T(4,128)S(1)}, f32[64,128,128]{2,1,0:T(8,128)}) while((s32[]{:T(128)}, f32[4,260,2,8,128]{4,3,2,1,0:T(8,128)}, f32[4,260,2,8,128]{4,3,2,1,0:T(8,128)}, s32[4,260]{1,0:T(4,128)S(1)}, ...), condition=%wide.region_6.7_spmd.clone, body=%wide.region_5.6_spmd.sunk.clone | while | flops 817891072 | bytes 55387264 | solution.py:99
  206.7 76.5 %all-to-all-done.2 = f32[4,260,2,8,128]{4,3,2,1,0:T(8,128)} async-done(((f32[4,260,2,8,128]{4,3,2,1,0:T(8,128)}), f32[4,260,2,8,128]{4,3,2,1,0:T(8,128)}, u32[]{:S(2)}, u32[]{:S(2)}) %all-to-all-start.2) | async-done | bytes 8519712 | tf_op jit(solution)/shard_map/all_to_all | solution.py:100
  295.3 283.1 %while.54 = (s32[]{:T(128)}, f32[9,128,8,8]{1,3,2,0:T(8,128)S(1)}, f32[128,65,128]{2,0,1:T(8,128)}, f32[128,65,2,128]{3,0,1,2:T(8,128)}, s32[128,2]{0,1:T(2,128)...) while((s32[]{:T(128)}, f32[9,128,8,8]{1,3,2,0:T(8,128)S(1)}, ...), condition=%wide.region_8.9_spmd.clone.clone, body=%wide.region_7.8_spmd.clone.sunk.clone | while | flops 1663609216 | bytes 68392240 | solution.py:115
  297.9 19.7 %multiply_add_fusion.8 = (f32[128,65,1,128]{3,0,1,2:T(8,128)S(1)}, f32[128,65,1,128]{3,0,1,2:T(8,128)S(1)}) fusion(f32[128,65,2,128]{3,0,1,2:T(8,128)} %get-tuple-element.828, s32[128]{0:T(128)S(1)} %get-tuple-element.740, s32[65,128]{1,0:T(8,128)S(1)} %get-tuple-element.741, s32[128]{0:T(128)S(1)} %get-tuple-element.742, ...), kind=kLoop, calls=%fused_computation.24.clone.1.clone | loop fusion | flops 23429120 | bytes 17106944 | tf_op jit(solution)/shard_map/while/body/eval_jaxpr/add | solution.py:35
  329.4 19.7 %multiply_add_fusion.8 = (f32[128,65,1,128]{3,0,1,2:T(8,128)S(1)}, f32[128,65,1,128]{3,0,1,2:T(8,128)S(1)}) fusion(f32[128,65,2,128]{3,0,1,2:T(8,128)} %get-tuple-element.828, s32[128]{0:T(128)S(1)} %get-tuple-element.740, s32[65,128]{1,0:T(8,128)S(1)} %get-tuple-element.741, s32[128]{0:T(128)S(1)} %get-tuple-element.742, ...), kind=kLoop, calls=%fused_computation.24.clone.1.clone | loop fusion | flops 23429120 | bytes 17106944 | tf_op jit(solution)/shard_map/while/body/eval_jaxpr/add | solution.py:35
  360.8 19.7 %multiply_add_fusion.8 = (f32[128,65,1,128]{3,0,1,2:T(8,128)S(1)}, f32[128,65,1,128]{3,0,1,2:T(8,128)S(1)}) fusion(f32[128,65,2,128]{3,0,1,2:T(8,128)} %get-tuple-element.828, s32[128]{0:T(128)S(1)} %get-tuple-element.740, s32[65,128]{1,0:T(8,128)S(1)} %get-tuple-element.741, s32[128]{0:T(128)S(1)} %get-tuple-element.742, ...), kind=kLoop, calls=%fused_computation.24.clone.1.clone | loop fusion | flops 23429120 | bytes 17106944 | tf_op jit(solution)/shard_map/while/body/eval_jaxpr/add | solution.py:35
  392.3 19.7 %multiply_add_fusion.8 = (f32[128,65,1,128]{3,0,1,2:T(8,128)S(1)}, f32[128,65,1,128]{3,0,1,2:T(8,128)S(1)}) fusion(f32[128,65,2,128]{3,0,1,2:T(8,128)} %get-tuple-element.828, s32[128]{0:T(128)S(1)} %get-tuple-element.740, s32[65,128]{1,0:T(8,128)S(1)} %get-tuple-element.741, s32[128]{0:T(128)S(1)} %get-tuple-element.742, ...), kind=kLoop, calls=%fused_computation.24.clone.1.clone | loop fusion | flops 23429120 | bytes 17106944 | tf_op jit(solution)/shard_map/while/body/eval_jaxpr/add | solution.py:35
  423.7 19.7 %multiply_add_fusion.8 = (f32[128,65,1,128]{3,0,1,2:T(8,128)S(1)}, f32[128,65,1,128]{3,0,1,2:T(8,128)S(1)}) fusion(f32[128,65,2,128]{3,0,1,2:T(8,128)} %get-tuple-element.828, s32[128]{0:T(128)S(1)} %get-tuple-element.740, s32[65,128]{1,0:T(8,128)S(1)} %get-tuple-element.741, s32[128]{0:T(128)S(1)} %get-tuple-element.742, ...), kind=kLoop, calls=%fused_computation.24.clone.1.clone | loop fusion | flops 23429120 | bytes 17106944 | tf_op jit(solution)/shard_map/while/body/eval_jaxpr/add | solution.py:35
  455.1 19.7 %multiply_add_fusion.8 = (f32[128,65,1,128]{3,0,1,2:T(8,128)S(1)}, f32[128,65,1,128]{3,0,1,2:T(8,128)S(1)}) fusion(f32[128,65,2,128]{3,0,1,2:T(8,128)} %get-tuple-element.828, s32[128]{0:T(128)S(1)} %get-tuple-element.740, s32[65,128]{1,0:T(8,128)S(1)} %get-tuple-element.741, s32[128]{0:T(128)S(1)} %get-tuple-element.742, ...), kind=kLoop, calls=%fused_computation.24.clone.1.clone | loop fusion | flops 23429120 | bytes 17106944 | tf_op jit(solution)/shard_map/while/body/eval_jaxpr/add | solution.py:35
  486.6 19.7 %multiply_add_fusion.8 = (f32[128,65,1,128]{3,0,1,2:T(8,128)S(1)}, f32[128,65,1,128]{3,0,1,2:T(8,128)S(1)}) fusion(f32[128,65,2,128]{3,0,1,2:T(8,128)} %get-tuple-element.828, s32[128]{0:T(128)S(1)} %get-tuple-element.740, s32[65,128]{1,0:T(8,128)S(1)} %get-tuple-element.741, s32[128]{0:T(128)S(1)} %get-tuple-element.742, ...), kind=kLoop, calls=%fused_computation.24.clone.1.clone | loop fusion | flops 23429120 | bytes 17106944 | tf_op jit(solution)/shard_map/while/body/eval_jaxpr/add | solution.py:35
  518.0 19.7 %multiply_add_fusion.8 = (f32[128,65,1,128]{3,0,1,2:T(8,128)S(1)}, f32[128,65,1,128]{3,0,1,2:T(8,128)S(1)}) fusion(f32[128,65,2,128]{3,0,1,2:T(8,128)} %get-tuple-element.828, s32[128]{0:T(128)S(1)} %get-tuple-element.740, s32[65,128]{1,0:T(8,128)S(1)} %get-tuple-element.741, s32[128]{0:T(128)S(1)} %get-tuple-element.742, ...), kind=kLoop, calls=%fused_computation.24.clone.1.clone | loop fusion | flops 23429120 | bytes 17106944 | tf_op jit(solution)/shard_map/while/body/eval_jaxpr/add | solution.py:35
  585.3 40.4 %pmax.7 = f32[128]{0:T(128)S(1)} all-reduce(f32[128]{0:T(128)S(1)} %fusion.84), channel_id=1, replica_groups=mesh['vol'=4,'orient'=4,'dp'=2] {'vol','orient'}, use_global_device_ids=true, to_apply=%region_11.12 | all-reduce | flops 128 | bytes 1024 | tf_op jit(solution)/shard_map/pmax | solution.py:123
  625.8 36.7 %psum.7 = f32[128,8]{0,1:T(8,128)S(1)} all-reduce(f32[128,8]{0,1:T(8,128)S(1)} %fusion.83), channel_id=1, replica_groups=mesh['vol'=4,'orient'=4,'dp'=2] {'vol','orient'}, use_global_device_ids=true, to_apply=%region_13.14 | all-reduce | flops 1024 | bytes 8192 | tf_op jit(solution)/shard_map/psum | solution.py:125
  663.2 299.8 %while.55 = (s32[]{:T(128)}, f32[8,65,2,8,128]{4,0,3,2,1:T(8,128)}, f32[128,65,128]{2,0,1:T(8,128)}, f32[128,65,2,128]{3,0,2,1:T(8,128)}, s32[128,2]{0,1:T(2,128...) while((s32[]{:T(128)}, f32[8,65,2,8,128]{4,0,3,2,1:T(8,128)}, ...), condition=%wide.region_16.17_spmd.clone.clone, body=%wide.region_15.16_spmd.clone.sunk.clone | while | flops 1665739136 | bytes 38507784 | solution.py:141
  665.5 20.7 %multiply_add_fusion.9 = (f32[128,65,1,128]{3,0,2,1:T(8,128)}, f32[128,65,1,128]{3,0,2,1:T(8,128)}) fusion(f32[128,65,2,128]{3,0,2,1:T(8,128)} %get-tuple-element.855, s32[128]{0:T(128)S(1)} %get-tuple-element.771, s32[65,128]{1,0:T(8,128)S(1)} %get-tuple-element.772, s32[128]{0:T(128)S(1)} %get-tuple-element.773, ...), kind=kLoop, calls=%fused_computation.56.clone.1.clone | loop fusion | flops 23429120 | bytes 17106944 | tf_op jit(solution)/shard_map/while/body/eval_jaxpr/add | solution.py:35
  698.3 20.7 %multiply_add_fusion.9 = (f32[128,65,1,128]{3,0,2,1:T(8,128)}, f32[128,65,1,128]{3,0,2,1:T(8,128)}) fusion(f32[128,65,2,128]{3,0,2,1:T(8,128)} %get-tuple-element.855, s32[128]{0:T(128)S(1)} %get-tuple-element.771, s32[65,128]{1,0:T(8,128)S(1)} %get-tuple-element.772, s32[128]{0:T(128)S(1)} %get-tuple-element.773, ...), kind=kLoop, calls=%fused_computation.56.clone.1.clone | loop fusion | flops 23429120 | bytes 17106944 | tf_op jit(solution)/shard_map/while/body/eval_jaxpr/add | solution.py:35
  731.7 20.7 %multiply_add_fusion.9 = (f32[128,65,1,128]{3,0,2,1:T(8,128)}, f32[128,65,1,128]{3,0,2,1:T(8,128)}) fusion(f32[128,65,2,128]{3,0,2,1:T(8,128)} %get-tuple-element.855, s32[128]{0:T(128)S(1)} %get-tuple-element.771, s32[65,128]{1,0:T(8,128)S(1)} %get-tuple-element.772, s32[128]{0:T(128)S(1)} %get-tuple-element.773, ...), kind=kLoop, calls=%fused_computation.56.clone.1.clone | loop fusion | flops 23429120 | bytes 17106944 | tf_op jit(solution)/shard_map/while/body/eval_jaxpr/add | solution.py:35
  765.1 20.7 %multiply_add_fusion.9 = (f32[128,65,1,128]{3,0,2,1:T(8,128)}, f32[128,65,1,128]{3,0,2,1:T(8,128)}) fusion(f32[128,65,2,128]{3,0,2,1:T(8,128)} %get-tuple-element.855, s32[128]{0:T(128)S(1)} %get-tuple-element.771, s32[65,128]{1,0:T(8,128)S(1)} %get-tuple-element.772, s32[128]{0:T(128)S(1)} %get-tuple-element.773, ...), kind=kLoop, calls=%fused_computation.56.clone.1.clone | loop fusion | flops 23429120 | bytes 17106944 | tf_op jit(solution)/shard_map/while/body/eval_jaxpr/add | solution.py:35
  798.4 20.7 %multiply_add_fusion.9 = (f32[128,65,1,128]{3,0,2,1:T(8,128)}, f32[128,65,1,128]{3,0,2,1:T(8,128)}) fusion(f32[128,65,2,128]{3,0,2,1:T(8,128)} %get-tuple-element.855, s32[128]{0:T(128)S(1)} %get-tuple-element.771, s32[65,128]{1,0:T(8,128)S(1)} %get-tuple-element.772, s32[128]{0:T(128)S(1)} %get-tuple-element.773, ...), kind=kLoop, calls=%fused_computation.56.clone.1.clone | loop fusion | flops 23429120 | bytes 17106944 | tf_op jit(solution)/shard_map/while/body/eval_jaxpr/add | solution.py:35
  831.8 20.7 %multiply_add_fusion.9 = (f32[128,65,1,128]{3,0,2,1:T(8,128)}, f32[128,65,1,128]{3,0,2,1:T(8,128)}) fusion(f32[128,65,2,128]{3,0,2,1:T(8,128)} %get-tuple-element.855, s32[128]{0:T(128)S(1)} %get-tuple-element.771, s32[65,128]{1,0:T(8,128)S(1)} %get-tuple-element.772, s32[128]{0:T(128)S(1)} %get-tuple-element.773, ...), kind=kLoop, calls=%fused_computation.56.clone.1.clone | loop fusion | flops 23429120 | bytes 17106944 | tf_op jit(solution)/shard_map/while/body/eval_jaxpr/add | solution.py:35
  865.2 20.7 %multiply_add_fusion.9 = (f32[128,65,1,128]{3,0,2,1:T(8,128)}, f32[128,65,1,128]{3,0,2,1:T(8,128)}) fusion(f32[128,65,2,128]{3,0,2,1:T(8,128)} %get-tuple-element.855, s32[128]{0:T(128)S(1)} %get-tuple-element.771, s32[65,128]{1,0:T(8,128)S(1)} %get-tuple-element.772, s32[128]{0:T(128)S(1)} %get-tuple-element.773, ...), kind=kLoop, calls=%fused_computation.56.clone.1.clone | loop fusion | flops 23429120 | bytes 17106944 | tf_op jit(solution)/shard_map/while/body/eval_jaxpr/add | solution.py:35
  898.6 20.7 %multiply_add_fusion.9 = (f32[128,65,1,128]{3,0,2,1:T(8,128)}, f32[128,65,1,128]{3,0,2,1:T(8,128)}) fusion(f32[128,65,2,128]{3,0,2,1:T(8,128)} %get-tuple-element.855, s32[128]{0:T(128)S(1)} %get-tuple-element.771, s32[65,128]{1,0:T(8,128)S(1)} %get-tuple-element.772, s32[128]{0:T(128)S(1)} %get-tuple-element.773, ...), kind=kLoop, calls=%fused_computation.56.clone.1.clone | loop fusion | flops 23429120 | bytes 17106944 | tf_op jit(solution)/shard_map/while/body/eval_jaxpr/add | solution.py:35
  932.0 20.7 %multiply_add_fusion.9 = (f32[128,65,1,128]{3,0,2,1:T(8,128)}, f32[128,65,1,128]{3,0,2,1:T(8,128)}) fusion(f32[128,65,2,128]{3,0,2,1:T(8,128)} %get-tuple-element.855, s32[128]{0:T(128)S(1)} %get-tuple-element.771, s32[65,128]{1,0:T(8,128)S(1)} %get-tuple-element.772, s32[128]{0:T(128)S(1)} %get-tuple-element.773, ...), kind=kLoop, calls=%fused_computation.56.clone.1.clone | loop fusion | flops 23429120 | bytes 17106944 | tf_op jit(solution)/shard_map/while/body/eval_jaxpr/add | solution.py:35
  977.5 69.6 %scatter_fusion = f32[1040,3,8,128]{3,2,1,0:T(8,128)} fusion(f32[1040,3,8,128]{3,2,1,0:T(8,128)} %broadcast_in_dim.61, s32[520]{0:T(1024)S(1)} %fusion.92, f32[520,3,8,128]{3,2,1,0:T(8,128)} %pad_maximum_fusion), kind=kCustom, calls=%fused_computation.6 | custom fusion | bytes 19171360 | tf_op jit(solution)/shard_map/scatter | solution.py:147
  1053.5 124.3 %all-to-all-done.3 = f32[4,260,3,8,128]{4,3,2,1,0:T(8,128)} async-done(((f32[4,260,3,8,128]{4,3,2,1,0:T(8,128)}), f32[4,260,3,8,128]{4,3,2,1,0:T(8,128)}, u32[]{:S(2)}, u32[]{:S(2)}) %all-to-all-start.3) | async-done | bytes 12779552 | tf_op jit(solution)/shard_map/all_to_all | solution.py:151
  1177.8 182.0 %while.53 = (s32[]{:T(128)}, f32[4,260,3,8,128]{4,3,2,1,0:T(8,128)}, f32[4,260,3,8,128]{4,3,2,1,0:T(8,128)}, s32[4,260]{1,0:T(4,128)}, f32[64,128,128]{2,1,0:T(8,128)}) while((s32[]{:T(128)}, f32[4,260,3,8,128]{4,3,2,1,0:T(8,128)}, f32[4,260,3,8,128]{4,3,2,1,0:T(8,128)}, s32[4,260]{1,0:T(4,128)}, ...), condition=%wide.region_20.21_spmd.clone, body=%wide.region_19.20_spmd.sunk.clone | while | flops 1226835712 | bytes 57517184 | solution.py:152
  1193.3 30.2 %bitcast_dynamic-update-slice_fusion.7 = f32[4,260,3,8,128]{4,3,2,1,0:T(8,128)} fusion(f32[4,260,3,8,128]{4,3,2,1,0:T(8,128)} %get-tuple-element.867, s32[]{:T(128)} %get-tuple-element.866, f32[260,128,128]{2,1,0:T(8,128)} %gather_fusion.1, f32[4,260,3,8,128]{4,3,2,1,0:T(8,128)} %get-tuple-element.873), kind=kOutput, calls=%fused_computation.87.clone.1.clone | convolution fusion | flops 1226833920 | bytes 23430144 | tf_op jit(solution)/shard_map/while/body/eval_jaxpr/nmkq,nrq->nmkr/dot_general | solution.py:47
  1238.9 30.2 %bitcast_dynamic-update-slice_fusion.7 = f32[4,260,3,8,128]{4,3,2,1,0:T(8,128)} fusion(f32[4,260,3,8,128]{4,3,2,1,0:T(8,128)} %get-tuple-element.867, s32[]{:T(128)} %get-tuple-element.866, f32[260,128,128]{2,1,0:T(8,128)} %gather_fusion.1, f32[4,260,3,8,128]{4,3,2,1,0:T(8,128)} %get-tuple-element.873), kind=kOutput, calls=%fused_computation.87.clone.1.clone | convolution fusion | flops 1226833920 | bytes 23430144 | tf_op jit(solution)/shard_map/while/body/eval_jaxpr/nmkq,nrq->nmkr/dot_general | solution.py:47
  1284.2 30.2 %bitcast_dynamic-update-slice_fusion.7 = f32[4,260,3,8,128]{4,3,2,1,0:T(8,128)} fusion(f32[4,260,3,8,128]{4,3,2,1,0:T(8,128)} %get-tuple-element.867, s32[]{:T(128)} %get-tuple-element.866, f32[260,128,128]{2,1,0:T(8,128)} %gather_fusion.1, f32[4,260,3,8,128]{4,3,2,1,0:T(8,128)} %get-tuple-element.873), kind=kOutput, calls=%fused_computation.87.clone.1.clone | convolution fusion | flops 1226833920 | bytes 23430144 | tf_op jit(solution)/shard_map/while/body/eval_jaxpr/nmkq,nrq->nmkr/dot_general | solution.py:47
  1329.5 30.2 %bitcast_dynamic-update-slice_fusion.7 = f32[4,260,3,8,128]{4,3,2,1,0:T(8,128)} fusion(f32[4,260,3,8,128]{4,3,2,1,0:T(8,128)} %get-tuple-element.867, s32[]{:T(128)} %get-tuple-element.866, f32[260,128,128]{2,1,0:T(8,128)} %gather_fusion.1, f32[4,260,3,8,128]{4,3,2,1,0:T(8,128)} %get-tuple-element.873), kind=kOutput, calls=%fused_computation.87.clone.1.clone | convolution fusion | flops 1226833920 | bytes 23430144 | tf_op jit(solution)/shard_map/while/body/eval_jaxpr/nmkq,nrq->nmkr/dot_general | solution.py:47
  1368.4 144.0 %scatter_fusion.1 = f32[2080,3,8,128]{3,2,1,0:T(8,128)} fusion(f32[2080,3,8,128]{3,2,1,0:T(8,128)} %broadcast_in_dim.53, s32[1040]{0:T(1024)S(1)} %copy-done.7, f32[1040,3,8,128]{3,2,1,0:T(8,128)} %bitcast.202), kind=kCustom, calls=%fused_computation.7 | custom fusion | flops 3194880 | bytes 38342720 | tf_op jit(solution)/shard_map/scatter-add | solution.py:155
  1513.7 248.7 %reduce-scatter.2.cloned.1.call-done = f32[4,65,3,8,128]{4,3,2,1,0:T(8,128)} async-done(((f32[32,65,3,8,128]{4,3,2,1,0:T(8,128)}), f32[4,65,3,8,128]{4,3,2,1,0:T(8,128)}) %reduce-scatter.2.cloned.1.call-update) | async-done | bytes 3194896 | tf_op jit(solution)/shard_map/reduce_scatter | solution.py:157
  (244 shorter events, 516.3 us)
Async XLA Ops:
  16.5 10.7 all-to-all-start
  27.2 25.3 %all-to-all-start.1 = ((s32[4,1,260]{2,1,0:T(1,128)}), s32[4,1,260]{2,1,0:T(1,128)S(1)}, u32[]{:S(2)}, u32[]{:S(2)}) async-start(s32[4,1,260]{2,1,0:T(1,128)} %all_to_all.22), calls=%async_computation.1 | async-start | bytes 12288 | tf_op jit(solution)/shard_map/all_to_all | solution.py:94
  31.7 13.2 copy-start.6
  182.7 100.4 %all-to-all-start.2 = ((f32[4,260,2,8,128]{4,3,2,1,0:T(8,128)}), f32[4,260,2,8,128]{4,3,2,1,0:T(8,128)}, u32[]{:S(2)}, u32[]{:S(2)}) async-start(f32[4,260,2,8,128]{4,3,2,1,0:T(8,128)} %get-tuple-element.363), calls=%async_computation.2 | async-start | bytes 17039360 | tf_op jit(solution)/shard_map/all_to_all | solution.py:100
  188.8 8.1 slice-start
  188.8 8.1 slice-start.1
  188.8 8.1 slice-start.2
  196.9 4.6 copy-start.13
  196.9 4.6 copy-start.14
  196.9 4.6 copy-start.8
  289.6 3.5 copy-start.3
  297.9 19.7 %copy-start.1 = (f32[128,65,128]{2,0,1:T(8,128)S(1)}, f32[128,65,128]{2,0,1:T(8,128)}, u32[]{:S(2)}) copy-start(f32[128,65,128]{2,0,1:T(8,128)} %get-tuple-element.827) | copy-start | bytes 12779524 | tf_op jit(solution)/shard_map/while
  297.9 19.7 %copy-start.2 = (f32[8,65,2,8,128]{4,3,1,0,2:T(8,128)S(1)}, f32[8,65,2,8,128]{4,3,1,0,2:T(8,128)}, u32[]{:S(2)}) copy-start(f32[8,65,2,8,128]{4,3,1,0,2:T(8,128)} %get-tuple-element.831) | copy-start | bytes 12779524 | tf_op jit(solution)/shard_map/while
  329.4 19.7 %copy-start.1 = (f32[128,65,128]{2,0,1:T(8,128)S(1)}, f32[128,65,128]{2,0,1:T(8,128)}, u32[]{:S(2)}) copy-start(f32[128,65,128]{2,0,1:T(8,128)} %get-tuple-element.827) | copy-start | bytes 12779524 | tf_op jit(solution)/shard_map/while
  329.4 19.7 %copy-start.2 = (f32[8,65,2,8,128]{4,3,1,0,2:T(8,128)S(1)}, f32[8,65,2,8,128]{4,3,1,0,2:T(8,128)}, u32[]{:S(2)}) copy-start(f32[8,65,2,8,128]{4,3,1,0,2:T(8,128)} %get-tuple-element.831) | copy-start | bytes 12779524 | tf_op jit(solution)/shard_map/while
  360.8 19.7 %copy-start.1 = (f32[128,65,128]{2,0,1:T(8,128)S(1)}, f32[128,65,128]{2,0,1:T(8,128)}, u32[]{:S(2)}) copy-start(f32[128,65,128]{2,0,1:T(8,128)} %get-tuple-element.827) | copy-start | bytes 12779524 | tf_op jit(solution)/shard_map/while
  360.8 19.7 %copy-start.2 = (f32[8,65,2,8,128]{4,3,1,0,2:T(8,128)S(1)}, f32[8,65,2,8,128]{4,3,1,0,2:T(8,128)}, u32[]{:S(2)}) copy-start(f32[8,65,2,8,128]{4,3,1,0,2:T(8,128)} %get-tuple-element.831) | copy-start | bytes 12779524 | tf_op jit(solution)/shard_map/while
  392.2 19.7 %copy-start.1 = (f32[128,65,128]{2,0,1:T(8,128)S(1)}, f32[128,65,128]{2,0,1:T(8,128)}, u32[]{:S(2)}) copy-start(f32[128,65,128]{2,0,1:T(8,128)} %get-tuple-element.827) | copy-start | bytes 12779524 | tf_op jit(solution)/shard_map/while
  392.2 19.7 %copy-start.2 = (f32[8,65,2,8,128]{4,3,1,0,2:T(8,128)S(1)}, f32[8,65,2,8,128]{4,3,1,0,2:T(8,128)}, u32[]{:S(2)}) copy-start(f32[8,65,2,8,128]{4,3,1,0,2:T(8,128)} %get-tuple-element.831) | copy-start | bytes 12779524 | tf_op jit(solution)/shard_map/while
  423.7 19.7 %copy-start.1 = (f32[128,65,128]{2,0,1:T(8,128)S(1)}, f32[128,65,128]{2,0,1:T(8,128)}, u32[]{:S(2)}) copy-start(f32[128,65,128]{2,0,1:T(8,128)} %get-tuple-element.827) | copy-start | bytes 12779524 | tf_op jit(solution)/shard_map/while
  423.7 19.7 %copy-start.2 = (f32[8,65,2,8,128]{4,3,1,0,2:T(8,128)S(1)}, f32[8,65,2,8,128]{4,3,1,0,2:T(8,128)}, u32[]{:S(2)}) copy-start(f32[8,65,2,8,128]{4,3,1,0,2:T(8,128)} %get-tuple-element.831) | copy-start | bytes 12779524 | tf_op jit(solution)/shard_map/while
  455.1 19.7 %copy-start.1 = (f32[128,65,128]{2,0,1:T(8,128)S(1)}, f32[128,65,128]{2,0,1:T(8,128)}, u32[]{:S(2)}) copy-start(f32[128,65,128]{2,0,1:T(8,128)} %get-tuple-element.827) | copy-start | bytes 12779524 | tf_op jit(solution)/shard_map/while
  455.1 19.7 %copy-start.2 = (f32[8,65,2,8,128]{4,3,1,0,2:T(8,128)S(1)}, f32[8,65,2,8,128]{4,3,1,0,2:T(8,128)}, u32[]{:S(2)}) copy-start(f32[8,65,2,8,128]{4,3,1,0,2:T(8,128)} %get-tuple-element.831) | copy-start | bytes 12779524 | tf_op jit(solution)/shard_map/while
  486.6 19.7 %copy-start.1 = (f32[128,65,128]{2,0,1:T(8,128)S(1)}, f32[128,65,128]{2,0,1:T(8,128)}, u32[]{:S(2)}) copy-start(f32[128,65,128]{2,0,1:T(8,128)} %get-tuple-element.827) | copy-start | bytes 12779524 | tf_op jit(solution)/shard_map/while
  486.6 19.7 %copy-start.2 = (f32[8,65,2,8,128]{4,3,1,0,2:T(8,128)S(1)}, f32[8,65,2,8,128]{4,3,1,0,2:T(8,128)}, u32[]{:S(2)}) copy-start(f32[8,65,2,8,128]{4,3,1,0,2:T(8,128)} %get-tuple-element.831) | copy-start | bytes 12779524 | tf_op jit(solution)/shard_map/while
  518.0 19.7 %copy-start.1 = (f32[128,65,128]{2,0,1:T(8,128)S(1)}, f32[128,65,128]{2,0,1:T(8,128)}, u32[]{:S(2)}) copy-start(f32[128,65,128]{2,0,1:T(8,128)} %get-tuple-element.827) | copy-start | bytes 12779524 | tf_op jit(solution)/shard_map/while
  518.0 19.7 %copy-start.2 = (f32[8,65,2,8,128]{4,3,1,0,2:T(8,128)S(1)}, f32[8,65,2,8,128]{4,3,1,0,2:T(8,128)}, u32[]{:S(2)}) copy-start(f32[8,65,2,8,128]{4,3,1,0,2:T(8,128)} %get-tuple-element.831) | copy-start | bytes 12779524 | tf_op jit(solution)/shard_map/while
  549.4 19.7 %copy-start.1 = (f32[128,65,128]{2,0,1:T(8,128)S(1)}, f32[128,65,128]{2,0,1:T(8,128)}, u32[]{:S(2)}) copy-start(f32[128,65,128]{2,0,1:T(8,128)} %get-tuple-element.827) | copy-start | bytes 12779524 | tf_op jit(solution)/shard_map/while
  549.5 19.7 %copy-start.2 = (f32[8,65,2,8,128]{4,3,1,0,2:T(8,128)S(1)}, f32[8,65,2,8,128]{4,3,1,0,2:T(8,128)}, u32[]{:S(2)}) copy-start(f32[8,65,2,8,128]{4,3,1,0,2:T(8,128)} %get-tuple-element.831) | copy-start | bytes 12779524 | tf_op jit(solution)/shard_map/while
  1047.1 130.7 %all-to-all-start.3 = ((f32[4,260,3,8,128]{4,3,2,1,0:T(8,128)}), f32[4,260,3,8,128]{4,3,2,1,0:T(8,128)}, u32[]{:S(2)}, u32[]{:S(2)}) async-start(f32[4,260,3,8,128]{4,3,2,1,0:T(8,128)} %bitcast.196), calls=%async_computation.3 | async-start | bytes 25559040 | tf_op jit(solution)/shard_map/all_to_all | solution.py:151
  1053.4 709.0 %reduce-scatter.2.cloned.1.call-start = ((), (), s32[]{:S(2)}) async-start(), calls=%async_computation.5 | async-start | bytes 28753920 | tf_op jit(solution)/shard_map/reduce_scatter | solution.py:157
  1359.7 8.7 copy-start.7
  (7 other events, 8.9 us)
Sparse Core Ops, SparseCore 0:
  1512.6 249.7 reduce-scatter.1
where the time goes:
time: 1780 us; the launch traced here: 1770 us
  other arithmetic  535 us (30%)
  waiting for transfers between devices  449 us (25%)
  matrix products  376 us (21%)
  local copies, waits for them, and re-layouts  261 us (15%)
  blocking collectives  77.1 us (4%)
  loops' own time  34 us (2%)
  starting transfers between devices  22 us (1%)
    add x18, other arithmetic, moved_images(): real_part * cosine + imag_part * sine_part  363 us
    reduce_scatter x1, waiting for transfers between devices, shards(): lax.psum_scatter(accumulated, ('orient', 'dp'), scatter_dimension=0, tile...  249 us
    scatter-add x1, other arithmetic, shards(): accumulated.at[cell_index]  144 us
    all_to_all x1, waiting for transfers between devices, shards(): lax.all_to_all(outgoing, 'vol', split_axis=0, concat_axis=0, tiled=True)  124 us
    dot_general x4, matrix products, back_project(): return jnp.einsum('nmkq,nrq->nmkr', tile_rows, matrices, precision=PRECISE)  121 us
    dot_general x9, matrix products, add_step(): jnp.einsum('ikp,itcq->ptckq', share_step, ctf[:, :, None, :] * moved, pre...  92.9 us
    dot_general x9, matrix products, score_step(): jnp.einsum('itcq,ptckq->ikp', ctf_noise[:, :, None, :] * moved, slices, p...  81.5 us
    all_to_all x1, waiting for transfers between devices, shards(): lax.all_to_all(pieces, 'vol', split_axis=0, concat_axis=0, tiled=True)  76.5 us
  transfers between devices with their start and end apart: 5, of which 3 were waited for; matrix products, arithmetic and copies ran while one was open for 2% of the time, Pallas kernels for 0%

commit v1 on v0

--- a/solution.py
+++ b/solution.py
@@ -97,7 +97,19 @@
     picked = flat_volume[jnp.maximum(incoming, 0)]
     blocks = jnp.where(is_valid[..., None, None, None], picked, 0.0)
     pieces = lax.map(project_group, (blocks, incoming_weight))
-    returned = lax.all_to_all(pieces, "vol", split_axis=0, concat_axis=0, tiled=True)
+    ways, here = (lax.axis_size("vol"), lax.axis_index("vol"))
+    width = pieces.shape[0] // ways
+    shape = list(pieces.shape)
+    shape[0] = width
+    height = shape[0]
+    shape[0] = height * ways
+    full = jnp.zeros(shape, pieces.dtype)
+    for mask in range(ways):
+        part = lax.dynamic_slice_in_dim(pieces, (here ^ mask) * width, width, axis=0)
+        if mask:
+            part = lax.ppermute(part, "vol", [(d, d ^ mask) for d in range(ways)])
+        full = lax.dynamic_update_slice_in_dim(full, part, (here ^ mask) * height, axis=0)
+    returned = full
     slices = returned.reshape(slab_count * capacity, 2, class_labels, tile_width)[slot_index]
     slices = slices.reshape(pose_local, tile_count, 2, class_labels, tile_width)
     freq_x, freq_y = pixel_frequencies(SIDE, tile_count, tile_width)

time: 1780 us -> 1790 us (level)
  local copies, waits for them, and re-layouts: 261 us -> 283 us
    all_to_all x1 -> x0, waiting for transfers between devices: 76.5 us -> none  [shards(): lax.all_to_all(pieces, 'vol', split_axis=0, concat_axis=0, tiled=True)]
    ppermute x0 -> x3, waiting for transfers between devices: none -> 69.2 us  [shards(): part = lax.ppermute(part, 'vol', [(d, d ^ mask) for d in range(ways)])]
  transfers between devices with their start and end apart: 5 -> 7, of which waited for: 3 -> 4; matrix products, arithmetic and copies ran while one was open for 2% -> 3% of each run, Pallas kernels for 0% -> 0%
where the time goes in v1:
time: 1790 us; the launch traced here: 1780 us
  other arithmetic  535 us (30%)
  waiting for transfers between devices  438 us (24%)
  matrix products  376 us (21%)
  local copies, waits for them, and re-layouts  283 us (16%)
  blocking collectives  78.8 us (4%)
  loops' own time  37 us (2%)
  starting transfers between devices  20.7 us (1%)
    add x18, other arithmetic, moved_images(): real_part * cosine + imag_part * sine_part  363 us
    reduce_scatter x1, waiting for transfers between devices, shards(): lax.psum_scatter(accumulated, ('orient', 'dp'), scatter_dimension=0, tile...  249 us
    scatter-add x1, other arithmetic, shards(): accumulated.at[cell_index]  144 us
    dot_general x4, matrix products, back_project(): return jnp.einsum('nmkq,nrq->nmkr', tile_rows, matrices, precision=PRECISE)  121 us
    all_to_all x1, waiting for transfers between devices, shards(): lax.all_to_all(outgoing, 'vol', split_axis=0, concat_axis=0, tiled=True)  120 us
    dot_general x9, matrix products, add_step(): jnp.einsum('ikp,itcq->ptckq', share_step, ctf[:, :, None, :] * moved, pre...  92.9 us
    dot_general x9, matrix products, score_step(): jnp.einsum('itcq,ptckq->ikp', ctf_noise[:, :, None, :] * moved, slices, p...  81.5 us
    dot_general x4, matrix products, project_tiles(): return jnp.einsum('nckr,nrq->nckq', blocks, matrices, precision=PRECISE)  71.5 us
  transfers between devices with their start and end apart: 7, of which 4 were waited for; matrix products, arithmetic and copies ran while one was open for 3% of the time, Pallas kernels for 0%

profile of v1, /device:TPU:0, one launch (start us, length us, event | category | flops | bytes accessed | tf_op | source)
XLA Modules:
  0.0 1784.3 jit_solution(18035411553375272944)
XLA Ops:
  56.4 130.1 %while.48 = (s32[]{:T(128)}, f32[4,260,2,8,128]{4,3,2,1,0:T(8,128)}, f32[4,260,2,8,128]{4,3,2,1,0:T(8,128)}, s32[4,260]{1,0:T(4,128)S(1)}, f32[64,128,128]{2,1,0:T(8,128)}, /*index=5*/s32[]{:T(128)}) while((s32[]{:T(128)}, f32[4,260,2,8,128]{4,3,2,1,0:T(8,128)}, f32[4,260,2,8,128]{4,3,2,1,0:T(8,128)}, s32[4,260]{1,0:T(4,128)S(1)}, ...), condition=%wide.region_6.7_spmd, body=%wide.region_5.6_spmd.sunk | while | flops 817891072 | bytes 55387272 | solution.py:99
  218.6 27.0 %collective-permute-done = f32[1,260,2,8,128]{4,3,2,1,0:T(8,128)} collective-permute-done((f32[1,260,2,8,128]{4,3,2,1,0:T(8,128)}, f32[1,260,2,8,128]{4,3,2,1,0:T(8,128)}, u32[]{:S(2)}, u32[]{:S(2)}) %collective-permute-start) | collective-permute-done | bytes 2129952 | tf_op jit(solution)/shard_map/ppermute | solution.py:110
  248.6 42.3 %collective-permute-done.1 = f32[1,260,2,8,128]{4,3,2,1,0:T(8,128)} collective-permute-done((f32[1,260,2,8,128]{4,3,2,1,0:T(8,128)}, f32[1,260,2,8,128]{4,3,2,1,0:T(8,128)}, u32[]{:S(2)}, u32[]{:S(2)}) %collective-permute-start.1) | collective-permute-done | bytes 2129952 | tf_op jit(solution)/shard_map/ppermute | solution.py:110
  309.3 283.1 %while.50 = (s32[]{:T(128)}, f32[9,128,8,8]{1,3,2,0:T(8,128)S(1)}, f32[128,65,128]{2,0,1:T(8,128)}, f32[128,65,2,128]{3,0,1,2:T(8,128)}, s32[128,2]{0,1:T(2,128)...) while((s32[]{:T(128)}, f32[9,128,8,8]{1,3,2,0:T(8,128)S(1)}, ...), condition=%wide.region_8.9_spmd.clone, body=%wide.region_7.8_spmd.clone.sunk | while | flops 1663609216 | bytes 68392272 | solution.py:127
  312.0 19.7 %multiply_add_fusion.6 = (f32[128,65,1,128]{3,0,1,2:T(8,128)S(1)}, f32[128,65,1,128]{3,0,1,2:T(8,128)S(1)}) fusion(f32[128,65,2,128]{3,0,1,2:T(8,128)} %get-tuple-element.757, s32[128]{0:T(128)S(1)} %get-tuple-element.691, s32[65,128]{1,0:T(8,128)S(1)} %get-tuple-element.692, s32[128]{0:T(128)S(1)} %get-tuple-element.693, ...), kind=kLoop, calls=%fused_computation.24.clone.1 | loop fusion | flops 23429120 | bytes 17106944 | tf_op jit(solution)/shard_map/while/body/eval_jaxpr/add | solution.py:35
  343.4 19.7 %multiply_add_fusion.6 = (f32[128,65,1,128]{3,0,1,2:T(8,128)S(1)}, f32[128,65,1,128]{3,0,1,2:T(8,128)S(1)}) fusion(f32[128,65,2,128]{3,0,1,2:T(8,128)} %get-tuple-element.757, s32[128]{0:T(128)S(1)} %get-tuple-element.691, s32[65,128]{1,0:T(8,128)S(1)} %get-tuple-element.692, s32[128]{0:T(128)S(1)} %get-tuple-element.693, ...), kind=kLoop, calls=%fused_computation.24.clone.1 | loop fusion | flops 23429120 | bytes 17106944 | tf_op jit(solution)/shard_map/while/body/eval_jaxpr/add | solution.py:35
  374.9 19.7 %multiply_add_fusion.6 = (f32[128,65,1,128]{3,0,1,2:T(8,128)S(1)}, f32[128,65,1,128]{3,0,1,2:T(8,128)S(1)}) fusion(f32[128,65,2,128]{3,0,1,2:T(8,128)} %get-tuple-element.757, s32[128]{0:T(128)S(1)} %get-tuple-element.691, s32[65,128]{1,0:T(8,128)S(1)} %get-tuple-element.692, s32[128]{0:T(128)S(1)} %get-tuple-element.693, ...), kind=kLoop, calls=%fused_computation.24.clone.1 | loop fusion | flops 23429120 | bytes 17106944 | tf_op jit(solution)/shard_map/while/body/eval_jaxpr/add | solution.py:35
  406.3 19.7 %multiply_add_fusion.6 = (f32[128,65,1,128]{3,0,1,2:T(8,128)S(1)}, f32[128,65,1,128]{3,0,1,2:T(8,128)S(1)}) fusion(f32[128,65,2,128]{3,0,1,2:T(8,128)} %get-tuple-element.757, s32[128]{0:T(128)S(1)} %get-tuple-element.691, s32[65,128]{1,0:T(8,128)S(1)} %get-tuple-element.692, s32[128]{0:T(128)S(1)} %get-tuple-element.693, ...), kind=kLoop, calls=%fused_computation.24.clone.1 | loop fusion | flops 23429120 | bytes 17106944 | tf_op jit(solution)/shard_map/while/body/eval_jaxpr/add | solution.py:35
  437.7 19.7 %multiply_add_fusion.6 = (f32[128,65,1,128]{3,0,1,2:T(8,128)S(1)}, f32[128,65,1,128]{3,0,1,2:T(8,128)S(1)}) fusion(f32[128,65,2,128]{3,0,1,2:T(8,128)} %get-tuple-element.757, s32[128]{0:T(128)S(1)} %get-tuple-element.691, s32[65,128]{1,0:T(8,128)S(1)} %get-tuple-element.692, s32[128]{0:T(128)S(1)} %get-tuple-element.693, ...), kind=kLoop, calls=%fused_computation.24.clone.1 | loop fusion | flops 23429120 | bytes 17106944 | tf_op jit(solution)/shard_map/while/body/eval_jaxpr/add | solution.py:35
  469.2 19.7 %multiply_add_fusion.6 = (f32[128,65,1,128]{3,0,1,2:T(8,128)S(1)}, f32[128,65,1,128]{3,0,1,2:T(8,128)S(1)}) fusion(f32[128,65,2,128]{3,0,1,2:T(8,128)} %get-tuple-element.757, s32[128]{0:T(128)S(1)} %get-tuple-element.691, s32[65,128]{1,0:T(8,128)S(1)} %get-tuple-element.692, s32[128]{0:T(128)S(1)} %get-tuple-element.693, ...), kind=kLoop, calls=%fused_computation.24.clone.1 | loop fusion | flops 23429120 | bytes 17106944 | tf_op jit(solution)/shard_map/while/body/eval_jaxpr/add | solution.py:35
  500.6 19.7 %multiply_add_fusion.6 = (f32[128,65,1,128]{3,0,1,2:T(8,128)S(1)}, f32[128,65,1,128]{3,0,1,2:T(8,128)S(1)}) fusion(f32[128,65,2,128]{3,0,1,2:T(8,128)} %get-tuple-element.757, s32[128]{0:T(128)S(1)} %get-tuple-element.691, s32[65,128]{1,0:T(8,128)S(1)} %get-tuple-element.692, s32[128]{0:T(128)S(1)} %get-tuple-element.693, ...), kind=kLoop, calls=%fused_computation.24.clone.1 | loop fusion | flops 23429120 | bytes 17106944 | tf_op jit(solution)/shard_map/while/body/eval_jaxpr/add | solution.py:35
  599.4 42.0 %pmax.7 = f32[128]{0:T(128)S(1)} all-reduce(f32[128]{0:T(128)S(1)} %fusion.84), channel_id=1, replica_groups=mesh['vol'=4,'orient'=4,'dp'=2] {'vol','orient'}, use_global_device_ids=true, to_apply=%region_11.12 | all-reduce | flops 128 | bytes 1024 | tf_op jit(solution)/shard_map/pmax | solution.py:135
  641.5 36.8 %psum.7 = f32[128,8]{0,1:T(8,128)S(1)} all-reduce(f32[128,8]{0,1:T(8,128)S(1)} %fusion.83), channel_id=1, replica_groups=mesh['vol'=4,'orient'=4,'dp'=2] {'vol','orient'}, use_global_device_ids=true, to_apply=%region_13.14 | all-reduce | flops 1024 | bytes 8192 | tf_op jit(solution)/shard_map/psum | solution.py:137
  679.0 302.8 %while.51 = (s32[]{:T(128)}, f32[8,65,2,8,128]{4,0,3,2,1:T(8,128)}, f32[128,65,128]{2,0,1:T(8,128)}, f32[128,65,2,128]{3,0,2,1:T(8,128)}, s32[128,2]{0,1:T(2,128...) while((s32[]{:T(128)}, f32[8,65,2,8,128]{4,0,3,2,1:T(8,128)}, ...), condition=%wide.region_16.17_spmd.clone, body=%wide.region_15.16_spmd.clone.sunk | while | flops 1665739136 | bytes 38507816 | solution.py:153
  681.6 20.7 %multiply_add_fusion.7 = (f32[128,65,1,128]{3,0,2,1:T(8,128)}, f32[128,65,1,128]{3,0,2,1:T(8,128)}) fusion(f32[128,65,2,128]{3,0,2,1:T(8,128)} %get-tuple-element.796, s32[128]{0:T(128)S(1)} %get-tuple-element.704, s32[65,128]{1,0:T(8,128)S(1)} %get-tuple-element.705, s32[128]{0:T(128)S(1)} %get-tuple-element.706, s32[65,128]{1,0:T(8,128)S(1)} %get-tuple-element.707), kind=kLoop, calls=%fused_computation.56.clone.1 | loop fusion | flops 23429120 | bytes 17106944 | tf_op jit(solution)/shard_map/while/body/eval_jaxpr/add | solution.py:35
  714.7 20.7 %multiply_add_fusion.7 = (f32[128,65,1,128]{3,0,2,1:T(8,128)}, f32[128,65,1,128]{3,0,2,1:T(8,128)}) fusion(f32[128,65,2,128]{3,0,2,1:T(8,128)} %get-tuple-element.796, s32[128]{0:T(128)S(1)} %get-tuple-element.704, s32[65,128]{1,0:T(8,128)S(1)} %get-tuple-element.705, s32[128]{0:T(128)S(1)} %get-tuple-element.706, s32[65,128]{1,0:T(8,128)S(1)} %get-tuple-element.707), kind=kLoop, calls=%fused_computation.56.clone.1 | loop fusion | flops 23429120 | bytes 17106944 | tf_op jit(solution)/shard_map/while/body/eval_jaxpr/add | solution.py:35
  748.4 20.7 %multiply_add_fusion.7 = (f32[128,65,1,128]{3,0,2,1:T(8,128)}, f32[128,65,1,128]{3,0,2,1:T(8,128)}) fusion(f32[128,65,2,128]{3,0,2,1:T(8,128)} %get-tuple-element.796, s32[128]{0:T(128)S(1)} %get-tuple-element.704, s32[65,128]{1,0:T(8,128)S(1)} %get-tuple-element.705, s32[128]{0:T(128)S(1)} %get-tuple-element.706, s32[65,128]{1,0:T(8,128)S(1)} %get-tuple-element.707), kind=kLoop, calls=%fused_computation.56.clone.1 | loop fusion | flops 23429120 | bytes 17106944 | tf_op jit(solution)/shard_map/while/body/eval_jaxpr/add | solution.py:35
  782.1 20.7 %multiply_add_fusion.7 = (f32[128,65,1,128]{3,0,2,1:T(8,128)}, f32[128,65,1,128]{3,0,2,1:T(8,128)}) fusion(f32[128,65,2,128]{3,0,2,1:T(8,128)} %get-tuple-element.796, s32[128]{0:T(128)S(1)} %get-tuple-element.704, s32[65,128]{1,0:T(8,128)S(1)} %get-tuple-element.705, s32[128]{0:T(128)S(1)} %get-tuple-element.706, s32[65,128]{1,0:T(8,128)S(1)} %get-tuple-element.707), kind=kLoop, calls=%fused_computation.56.clone.1 | loop fusion | flops 23429120 | bytes 17106944 | tf_op jit(solution)/shard_map/while/body/eval_jaxpr/add | solution.py:35
  815.8 20.7 %multiply_add_fusion.7 = (f32[128,65,1,128]{3,0,2,1:T(8,128)}, f32[128,65,1,128]{3,0,2,1:T(8,128)}) fusion(f32[128,65,2,128]{3,0,2,1:T(8,128)} %get-tuple-element.796, s32[128]{0:T(128)S(1)} %get-tuple-element.704, s32[65,128]{1,0:T(8,128)S(1)} %get-tuple-element.705, s32[128]{0:T(128)S(1)} %get-tuple-element.706, s32[65,128]{1,0:T(8,128)S(1)} %get-tuple-element.707), kind=kLoop, calls=%fused_computation.56.clone.1 | loop fusion | flops 23429120 | bytes 17106944 | tf_op jit(solution)/shard_map/while/body/eval_jaxpr/add | solution.py:35
  849.5 20.7 %multiply_add_fusion.7 = (f32[128,65,1,128]{3,0,2,1:T(8,128)}, f32[128,65,1,128]{3,0,2,1:T(8,128)}) fusion(f32[128,65,2,128]{3,0,2,1:T(8,128)} %get-tuple-element.796, s32[128]{0:T(128)S(1)} %get-tuple-element.704, s32[65,128]{1,0:T(8,128)S(1)} %get-tuple-element.705, s32[128]{0:T(128)S(1)} %get-tuple-element.706, s32[65,128]{1,0:T(8,128)S(1)} %get-tuple-element.707), kind=kLoop, calls=%fused_computation.56.clone.1 | loop fusion | flops 23429120 | bytes 17106944 | tf_op jit(solution)/shard_map/while/body/eval_jaxpr/add | solution.py:35
  883.2 20.7 %multiply_add_fusion.7 = (f32[128,65,1,128]{3,0,2,1:T(8,128)}, f32[128,65,1,128]{3,0,2,1:T(8,128)}) fusion(f32[128,65,2,128]{3,0,2,1:T(8,128)} %get-tuple-element.796, s32[128]{0:T(128)S(1)} %get-tuple-element.704, s32[65,128]{1,0:T(8,128)S(1)} %get-tuple-element.705, s32[128]{0:T(128)S(1)} %get-tuple-element.706, s32[65,128]{1,0:T(8,128)S(1)} %get-tuple-element.707), kind=kLoop, calls=%fused_computation.56.clone.1 | loop fusion | flops 23429120 | bytes 17106944 | tf_op jit(solution)/shard_map/while/body/eval_jaxpr/add | solution.py:35
  916.9 20.7 %multiply_add_fusion.7 = (f32[128,65,1,128]{3,0,2,1:T(8,128)}, f32[128,65,1,128]{3,0,2,1:T(8,128)}) fusion(f32[128,65,2,128]{3,0,2,1:T(8,128)} %get-tuple-element.796, s32[128]{0:T(128)S(1)} %get-tuple-element.704, s32[65,128]{1,0:T(8,128)S(1)} %get-tuple-element.705, s32[128]{0:T(128)S(1)} %get-tuple-element.706, s32[65,128]{1,0:T(8,128)S(1)} %get-tuple-element.707), kind=kLoop, calls=%fused_computation.56.clone.1 | loop fusion | flops 23429120 | bytes 17106944 | tf_op jit(solution)/shard_map/while/body/eval_jaxpr/add | solution.py:35
  950.7 20.7 %multiply_add_fusion.7 = (f32[128,65,1,128]{3,0,2,1:T(8,128)}, f32[128,65,1,128]{3,0,2,1:T(8,128)}) fusion(f32[128,65,2,128]{3,0,2,1:T(8,128)} %get-tuple-element.796, s32[128]{0:T(128)S(1)} %get-tuple-element.704, s32[65,128]{1,0:T(8,128)S(1)} %get-tuple-element.705, s32[128]{0:T(128)S(1)} %get-tuple-element.706, s32[65,128]{1,0:T(8,128)S(1)} %get-tuple-element.707), kind=kLoop, calls=%fused_computation.56.clone.1 | loop fusion | flops 23429120 | bytes 17106944 | tf_op jit(solution)/shard_map/while/body/eval_jaxpr/add | solution.py:35
  996.2 69.6 %scatter_fusion = f32[1040,3,8,128]{3,2,1,0:T(8,128)} fusion(f32[1040,3,8,128]{3,2,1,0:T(8,128)} %broadcast_in_dim.59, s32[520]{0:T(1024)S(1)} %fusion.92, f32[520,3,8,128]{3,2,1,0:T(8,128)} %pad_maximum_fusion), kind=kCustom, calls=%fused_computation.6 | custom fusion | bytes 19171360 | tf_op jit(solution)/shard_map/scatter | solution.py:159
  1072.2 119.7 %all-to-all-done.2 = f32[4,260,3,8,128]{4,3,2,1,0:T(8,128)} async-done(((f32[4,260,3,8,128]{4,3,2,1,0:T(8,128)}), f32[4,260,3,8,128]{4,3,2,1,0:T(8,128)}, u32[]{:S(2)}, u32[]{:S(2)}) %all-to-all-start.2) | async-done | bytes 12779552 | tf_op jit(solution)/shard_map/all_to_all | solution.py:163
  1191.9 182.0 %while.49 = (s32[]{:T(128)}, f32[4,260,3,8,128]{4,3,2,1,0:T(8,128)}, f32[4,260,3,8,128]{4,3,2,1,0:T(8,128)}, s32[4,260]{1,0:T(4,128)}, f32[64,128,128]{2,1,0:T(8,128)}, /*index=5*/s32[]{:T(128)}) while((s32[]{:T(128)}, f32[4,260,3,8,128]{4,3,2,1,0:T(8,128)}, f32[4,260,3,8,128]{4,3,2,1,0:T(8,128)}, s32[4,260]{1,0:T(4,128)}, ...), condition=%wide.region_20.21_spmd, body=%wide.region_19.20_spmd.sunk | while | flops 1226835712 | bytes 57517192 | solution.py:164
  1207.4 30.2 %bitcast_dynamic-update-slice_fusion.5 = f32[4,260,3,8,128]{4,3,2,1,0:T(8,128)} fusion(f32[4,260,3,8,128]{4,3,2,1,0:T(8,128)} %get-tuple-element.813, s32[]{:T(128)} %get-tuple-element.812, f32[260,128,128]{2,1,0:T(8,128)} %gather_fusion.1, f32[4,260,3,8,128]{4,3,2,1,0:T(8,128)} %get-tuple-element.820), kind=kOutput, calls=%fused_computation.87.clone.1 | convolution fusion | flops 1226833920 | bytes 23430144 | tf_op jit(solution)/shard_map/while/body/eval_jaxpr/nmkq,nrq->nmkr/dot_general | solution.py:47
  1253.0 30.2 %bitcast_dynamic-update-slice_fusion.5 = f32[4,260,3,8,128]{4,3,2,1,0:T(8,128)} fusion(f32[4,260,3,8,128]{4,3,2,1,0:T(8,128)} %get-tuple-element.813, s32[]{:T(128)} %get-tuple-element.812, f32[260,128,128]{2,1,0:T(8,128)} %gather_fusion.1, f32[4,260,3,8,128]{4,3,2,1,0:T(8,128)} %get-tuple-element.820), kind=kOutput, calls=%fused_computation.87.clone.1 | convolution fusion | flops 1226833920 | bytes 23430144 | tf_op jit(solution)/shard_map/while/body/eval_jaxpr/nmkq,nrq->nmkr/dot_general | solution.py:47
  1298.3 30.2 %bitcast_dynamic-update-slice_fusion.5 = f32[4,260,3,8,128]{4,3,2,1,0:T(8,128)} fusion(f32[4,260,3,8,128]{4,3,2,1,0:T(8,128)} %get-tuple-element.813, s32[]{:T(128)} %get-tuple-element.812, f32[260,128,128]{2,1,0:T(8,128)} %gather_fusion.1, f32[4,260,3,8,128]{4,3,2,1,0:T(8,128)} %get-tuple-element.820), kind=kOutput, calls=%fused_computation.87.clone.1 | convolution fusion | flops 1226833920 | bytes 23430144 | tf_op jit(solution)/shard_map/while/body/eval_jaxpr/nmkq,nrq->nmkr/dot_general | solution.py:47
  1343.6 30.2 %bitcast_dynamic-update-slice_fusion.5 = f32[4,260,3,8,128]{4,3,2,1,0:T(8,128)} fusion(f32[4,260,3,8,128]{4,3,2,1,0:T(8,128)} %get-tuple-element.813, s32[]{:T(128)} %get-tuple-element.812, f32[260,128,128]{2,1,0:T(8,128)} %gather_fusion.1, f32[4,260,3,8,128]{4,3,2,1,0:T(8,128)} %get-tuple-element.820), kind=kOutput, calls=%fused_computation.87.clone.1 | convolution fusion | flops 1226833920 | bytes 23430144 | tf_op jit(solution)/shard_map/while/body/eval_jaxpr/nmkq,nrq->nmkr/dot_general | solution.py:47
  1382.5 144.0 %scatter_fusion.1 = f32[2080,3,8,128]{3,2,1,0:T(8,128)} fusion(f32[2080,3,8,128]{3,2,1,0:T(8,128)} %broadcast_in_dim.51, s32[1040]{0:T(1024)S(1)} %copy-done.9, f32[1040,3,8,128]{3,2,1,0:T(8,128)} %bitcast.181), kind=kCustom, calls=%fused_computation.7 | custom fusion | flops 3194880 | bytes 38342720 | tf_op jit(solution)/shard_map/scatter-add | solution.py:167
  1527.8 249.4 %reduce-scatter.2.cloned.1.call-done = f32[4,65,3,8,128]{4,3,2,1,0:T(8,128)} async-done(((f32[32,65,3,8,128]{4,3,2,1,0:T(8,128)}), f32[4,65,3,8,128]{4,3,2,1,0:T(8,128)}) %reduce-scatter.2.cloned.1.call-update) | async-done | bytes 3194896 | tf_op jit(solution)/shard_map/reduce_scatter | solution.py:169
  (257 shorter events, 557.1 us)
Async XLA Ops:
  16.5 10.7 all-to-all-start
  27.2 25.3 %all-to-all-start.1 = ((s32[4,1,260]{2,1,0:T(1,128)}), s32[4,1,260]{2,1,0:T(1,128)S(1)}, u32[]{:S(2)}, u32[]{:S(2)}) async-start(s32[4,1,260]{2,1,0:T(1,128)} %all_to_all.19), calls=%async_computation.1 | async-start | bytes 12288 | tf_op jit(solution)/shard_map/all_to_all | solution.py:94
  31.7 13.2 copy-start.8
  196.0 49.6 %collective-permute-start = (f32[1,260,2,8,128]{4,3,2,1,0:T(8,128)}, f32[1,260,2,8,128]{4,3,2,1,0:T(8,128)}, u32[]{:S(2)}, u32[]{:S(2)}) collective-permute-start(f32[1,260,2,8,128]{4,3,2,1,0:T(8,128)} %get-tuple-element.534), channel_id=1, source_target_pairs={{0,8},{8,0},{16,24},{24,16},{1,9},{9,1},{17,25},{25,17},{2,10},{10... | collective-permute-start | bytes 6389768 | tf_op jit(solution)/shard_map/ppermute | solution.py:110
  197.7 93.2 %collective-permute-start.1 = (f32[1,260,2,8,128]{4,3,2,1,0:T(8,128)}, f32[1,260,2,8,128]{4,3,2,1,0:T(8,128)}, u32[]{:S(2)}, u32[]{:S(2)}) collective-permute-start(f32[1,260,2,8,128]{4,3,2,1,0:T(8,128)} %get-tuple-element.533), channel_id=1, source_target_pairs={{0,16},{8,24},{16,0},{24,8},{1,17},{9,25},{17,1},{25,9},{2,18},{10... | collective-permute-start | bytes 6389768 | tf_op jit(solution)/shard_map/ppermute | solution.py:110
  200.8 93.2 %collective-permute-start.2 = (f32[1,260,2,8,128]{4,3,2,1,0:T(8,128)S(1)}, f32[1,260,2,8,128]{4,3,2,1,0:T(8,128)}, u32[]{:S(2)}, u32[]{:S(2)}) collective-permute-start(f32[1,260,2,8,128]{4,3,2,1,0:T(8,128)S(1)} %get-tuple-element.532), channel_id=1, source_target_pairs={{0,24},{8,16},{16,8},{24,0},{1,25},{9,17},{17,9},{25,1},{2,26},{10... | collective-permute-start | bytes 6389768 | tf_op jit(solution)/shard_map/ppermute | solution.py:110
  200.8 8.1 slice-start
  200.8 8.1 slice-start.1
  200.8 8.1 slice-start.2
  208.8 4.6 copy-start.15
  208.9 4.6 copy-start.10
  312.0 19.7 %copy-start.1 = (f32[128,65,128]{2,0,1:T(8,128)S(1)}, f32[128,65,128]{2,0,1:T(8,128)}, u32[]{:S(2)}) copy-start(f32[128,65,128]{2,0,1:T(8,128)} %get-tuple-element.756) | copy-start | bytes 12779524 | tf_op jit(solution)/shard_map/while
  312.0 19.7 %copy-start.2 = (f32[8,65,2,8,128]{4,3,1,0,2:T(8,128)S(1)}, f32[8,65,2,8,128]{4,3,1,0,2:T(8,128)}, u32[]{:S(2)}) copy-start(f32[8,65,2,8,128]{4,3,1,0,2:T(8,128)} %get-tuple-element.760) | copy-start | bytes 12779524 | tf_op jit(solution)/shard_map/while
  343.4 19.7 %copy-start.1 = (f32[128,65,128]{2,0,1:T(8,128)S(1)}, f32[128,65,128]{2,0,1:T(8,128)}, u32[]{:S(2)}) copy-start(f32[128,65,128]{2,0,1:T(8,128)} %get-tuple-element.756) | copy-start | bytes 12779524 | tf_op jit(solution)/shard_map/while
  343.4 19.7 %copy-start.2 = (f32[8,65,2,8,128]{4,3,1,0,2:T(8,128)S(1)}, f32[8,65,2,8,128]{4,3,1,0,2:T(8,128)}, u32[]{:S(2)}) copy-start(f32[8,65,2,8,128]{4,3,1,0,2:T(8,128)} %get-tuple-element.760) | copy-start | bytes 12779524 | tf_op jit(solution)/shard_map/while
  374.8 19.7 %copy-start.1 = (f32[128,65,128]{2,0,1:T(8,128)S(1)}, f32[128,65,128]{2,0,1:T(8,128)}, u32[]{:S(2)}) copy-start(f32[128,65,128]{2,0,1:T(8,128)} %get-tuple-element.756) | copy-start | bytes 12779524 | tf_op jit(solution)/shard_map/while
  374.8 19.7 %copy-start.2 = (f32[8,65,2,8,128]{4,3,1,0,2:T(8,128)S(1)}, f32[8,65,2,8,128]{4,3,1,0,2:T(8,128)}, u32[]{:S(2)}) copy-start(f32[8,65,2,8,128]{4,3,1,0,2:T(8,128)} %get-tuple-element.760) | copy-start | bytes 12779524 | tf_op jit(solution)/shard_map/while
  406.3 19.7 %copy-start.1 = (f32[128,65,128]{2,0,1:T(8,128)S(1)}, f32[128,65,128]{2,0,1:T(8,128)}, u32[]{:S(2)}) copy-start(f32[128,65,128]{2,0,1:T(8,128)} %get-tuple-element.756) | copy-start | bytes 12779524 | tf_op jit(solution)/shard_map/while
  406.3 19.7 %copy-start.2 = (f32[8,65,2,8,128]{4,3,1,0,2:T(8,128)S(1)}, f32[8,65,2,8,128]{4,3,1,0,2:T(8,128)}, u32[]{:S(2)}) copy-start(f32[8,65,2,8,128]{4,3,1,0,2:T(8,128)} %get-tuple-element.760) | copy-start | bytes 12779524 | tf_op jit(solution)/shard_map/while
  437.7 19.7 %copy-start.1 = (f32[128,65,128]{2,0,1:T(8,128)S(1)}, f32[128,65,128]{2,0,1:T(8,128)}, u32[]{:S(2)}) copy-start(f32[128,65,128]{2,0,1:T(8,128)} %get-tuple-element.756) | copy-start | bytes 12779524 | tf_op jit(solution)/shard_map/while
  437.7 19.7 %copy-start.2 = (f32[8,65,2,8,128]{4,3,1,0,2:T(8,128)S(1)}, f32[8,65,2,8,128]{4,3,1,0,2:T(8,128)}, u32[]{:S(2)}) copy-start(f32[8,65,2,8,128]{4,3,1,0,2:T(8,128)} %get-tuple-element.760) | copy-start | bytes 12779524 | tf_op jit(solution)/shard_map/while
  469.2 19.7 %copy-start.1 = (f32[128,65,128]{2,0,1:T(8,128)S(1)}, f32[128,65,128]{2,0,1:T(8,128)}, u32[]{:S(2)}) copy-start(f32[128,65,128]{2,0,1:T(8,128)} %get-tuple-element.756) | copy-start | bytes 12779524 | tf_op jit(solution)/shard_map/while
  469.2 19.7 %copy-start.2 = (f32[8,65,2,8,128]{4,3,1,0,2:T(8,128)S(1)}, f32[8,65,2,8,128]{4,3,1,0,2:T(8,128)}, u32[]{:S(2)}) copy-start(f32[8,65,2,8,128]{4,3,1,0,2:T(8,128)} %get-tuple-element.760) | copy-start | bytes 12779524 | tf_op jit(solution)/shard_map/while
  500.6 19.7 %copy-start.1 = (f32[128,65,128]{2,0,1:T(8,128)S(1)}, f32[128,65,128]{2,0,1:T(8,128)}, u32[]{:S(2)}) copy-start(f32[128,65,128]{2,0,1:T(8,128)} %get-tuple-element.756) | copy-start | bytes 12779524 | tf_op jit(solution)/shard_map/while
  500.6 19.7 %copy-start.2 = (f32[8,65,2,8,128]{4,3,1,0,2:T(8,128)S(1)}, f32[8,65,2,8,128]{4,3,1,0,2:T(8,128)}, u32[]{:S(2)}) copy-start(f32[8,65,2,8,128]{4,3,1,0,2:T(8,128)} %get-tuple-element.760) | copy-start | bytes 12779524 | tf_op jit(solution)/shard_map/while
  532.0 19.7 %copy-start.1 = (f32[128,65,128]{2,0,1:T(8,128)S(1)}, f32[128,65,128]{2,0,1:T(8,128)}, u32[]{:S(2)}) copy-start(f32[128,65,128]{2,0,1:T(8,128)} %get-tuple-element.756) | copy-start | bytes 12779524 | tf_op jit(solution)/shard_map/while
  532.0 19.7 %copy-start.2 = (f32[8,65,2,8,128]{4,3,1,0,2:T(8,128)S(1)}, f32[8,65,2,8,128]{4,3,1,0,2:T(8,128)}, u32[]{:S(2)}) copy-start(f32[8,65,2,8,128]{4,3,1,0,2:T(8,128)} %get-tuple-element.760) | copy-start | bytes 12779524 | tf_op jit(solution)/shard_map/while
  563.5 19.7 %copy-start.1 = (f32[128,65,128]{2,0,1:T(8,128)S(1)}, f32[128,65,128]{2,0,1:T(8,128)}, u32[]{:S(2)}) copy-start(f32[128,65,128]{2,0,1:T(8,128)} %get-tuple-element.756) | copy-start | bytes 12779524 | tf_op jit(solution)/shard_map/while
  563.5 19.7 %copy-start.2 = (f32[8,65,2,8,128]{4,3,1,0,2:T(8,128)S(1)}, f32[8,65,2,8,128]{4,3,1,0,2:T(8,128)}, u32[]{:S(2)}) copy-start(f32[8,65,2,8,128]{4,3,1,0,2:T(8,128)} %get-tuple-element.760) | copy-start | bytes 12779524 | tf_op jit(solution)/shard_map/while
  1065.8 126.1 %all-to-all-start.2 = ((f32[4,260,3,8,128]{4,3,2,1,0:T(8,128)}), f32[4,260,3,8,128]{4,3,2,1,0:T(8,128)}, u32[]{:S(2)}, u32[]{:S(2)}) async-start(f32[4,260,3,8,128]{4,3,2,1,0:T(8,128)} %bitcast.174), calls=%async_computation.2 | async-start | bytes 25559040 | tf_op jit(solution)/shard_map/all_to_all | solution.py:163
  1072.1 705.1 %reduce-scatter.2.cloned.1.call-start = ((), (), s32[]{:S(2)}) async-start(), calls=%async_computation.4 | async-start | bytes 28753920 | tf_op jit(solution)/shard_map/reduce_scatter | solution.py:169
  1373.8 8.7 copy-start.9
  (11 other events, 23.8 us)
Sparse Core Ops, SparseCore 0:
  1526.7 250.5 reduce-scatter.1
